TPU v7x, 32 devices: a whole 2x2x4 slice. The times are simulated.
32 devices in a mesh: term: 8 (over z, x), sector: 4 (over y, core).
Axes of the slice: x: 2, y: 2, z: 4, core: 2. Of those that a mesh axis runs over, the one named last changes fastest.
Arguments:
- psi_start: float32 [4, 384, 384], P('sector'), may hold values from -6 to 6
- diagonal: float32 [4, 384, 384], P('sector'), may hold values from -3 to 3
- left_ops: float32 [128, 384, 384], P(('term', 'sector')), may hold values from -0.3125 to 0.3125
- right_ops: float32 [128, 384, 384], P(('term', 'sector')), may hold values from -0.078125 to 0.078125
- pair_in: int32 [32, 4], P(('term', 'sector')), may hold values from 0 to 3
- pair_out: int32 [32, 4], P(('term', 'sector')), may hold values from 0 to 3
- pair_count: int32 [32], P(('term', 'sector')), may hold values from 1 to 4, as said below
Outputs:
- psi_final: float32 [4, 384, 384], P('sector')
- energies: float32 [2], replicated
Inputs may be any that keep to these rules, and one draw needn't show every extreme that they name: `pair_count`: some device has all 4 slots live in every draw.
All inputs are finite; a program needn't handle non-finite values.
Results may differ from a plain program's by a relative error of at most 0.00013.
Values sent between devices are 32-bit elements; how exact they have to be, the bound alone decides.
No kernel may reach another device: no remote copies, remote signals or barrier semaphores. Data moves between devices by JAX's collectives and lax.ppermute only.
A program may use at most 64 MiB of HBM per device.

v0:
```python
import jax
import jax.numpy as jnp
from jax import lax
from jax.sharding import PartitionSpec as P

ITERS = 2
epsilon = 1e-06


def apply_pairs(gathered, left_ops, right_ops, pair_in, pair_out, pair_count):

    def one_pair(pair_slot, partial_value):
        source = lax.dynamic_index_in_dim(gathered, pair_in[0, pair_slot], 0, keepdims=False)
        left_block = lax.dynamic_index_in_dim(left_ops, pair_slot, 0, keepdims=False)
        right_block = lax.dynamic_index_in_dim(right_ops, pair_slot, 0, keepdims=False)
        inner_prod = jnp.dot(left_block, source, precision=lax.Precision.HIGHEST)
        product = lax.dot_general(
            inner_prod, right_block, (((1,), (1,)), ((), ())), precision=lax.Precision.HIGHEST
        )
        target = pair_out[0, pair_slot]
        current = lax.dynamic_index_in_dim(partial_value, target, 0, keepdims=False)
        return lax.dynamic_update_index_in_dim(partial_value, current + product, target, 0)

    return lax.fori_loop(0, pair_count[0], one_pair, jnp.zeros(gathered.shape, jnp.float32))


def global_sums(values):
    return lax.psum((values[0],), "sector")


def sigma_blocks(vector, left_ops, right_ops, pair_in, pair_out, pair_count):
    gathered = lax.all_gather(vector, "sector", axis=0, tiled=True)
    partial_value = apply_pairs(gathered, left_ops, right_ops, pair_in, pair_out, pair_count)
    owned_sum = lax.psum_scatter(partial_value, "sector", scatter_dimension=0, tiled=True)
    return lax.psum(owned_sum, "term")


def shards(psi_start, diagonal, left_ops, right_ops, pair_in, pair_out, pair_count):
    vector = psi_start
    cell_total = float(
        psi_start.shape[0] * lax.axis_size("sector") * psi_start.shape[1] * psi_start.shape[2]
    )
    energies = []
    for sweep in range(ITERS):
        vec_share = vector
        squares = global_sums((jnp.sum(vec_share * vec_share),))[0]
        inverse_norm = 1.0 / jnp.sqrt(squares / cell_total + epsilon)
        normed = vector * inverse_norm
        sigma = sigma_blocks(normed, left_ops, right_ops, pair_in, pair_out, pair_count)
        product_sum = global_sums((jnp.sum(normed * sigma),))[0]
        rayleigh = product_sum / cell_total
        residual = sigma - rayleigh * normed
        correction = residual / jnp.maximum(jnp.abs(diagonal - rayleigh), 1.0)
        updated = normed - correction
        vector = updated
        energies.append(rayleigh)
    return (vector, jnp.stack(energies))


def solution(mesh):
    return jax.shard_map(
        shards,
        mesh=mesh,
        in_specs=(
            P("sector", None, None),
            P("sector", None, None),
            P(("term", "sector"), None, None),
            P(("term", "sector"), None, None),
            P(("term", "sector"), None),
            P(("term", "sector"), None),
            P(("term", "sector")),
        ),
        out_specs=(P("sector", None, None), P()),
        check_vma=False,
    )
```

profile of v0, /device:TPU:0, one launch (start us, length us, event | category | flops | bytes accessed | tf_op | source)
XLA Modules:
  0.0 407.2 jit_solution(11676332899711747829)
XLA Ops:
  7.2 1.8 multiply_reduce_fusion.3
  9.1 9.0 %psum.42 = f32[]{:T(128)} all-reduce(f32[]{:T(128)} %multiply_reduce_fusion.3), channel_id=1, replica_groups=mesh['term'=8,'sector'=4] {'sector'}, use_global_device_ids=true, to_apply=%region_1.0 | all-reduce | flops 1 | bytes 8 | tf_op jit(solution)/shard_map/psum | solution.py:28
  18.7 1.9 broadcast_multiply_fusion.1
  20.7 24.4 %all-gather.3.cloned.1.call-done = f32[4,384,384]{2,1,0:T(8,128)} async-done(((f32[1,384,384]{2,1,0:T(8,128)}), f32[4,384,384]{2,1,0:T(8,128)}) %all-gather.3.cloned.1.call-update) | async-done | bytes 2359312 | tf_op jit(solution)/shard_map/all_gather | solution.py:32
  45.2 0.2 broadcast.6.clone
  45.4 39.8 %while.20 = (s32[]{:T(128)}, f32[4,384,384]{2,1,0:T(8,128)S(1)}, s32[]{:T(128)}, s32[1,4]{1,0:T(1,128)S(1)}, f32[4,384,384]{2,1,0:T(8,128)}, /*index=5*/s32[1,4]...) while((s32[]{:T(128)}, f32[4,384,384]{2,1,0:T(8,128)S(1)}, ...), condition=%wide.region_3.4_spmd, body=%wide.region_2.3_spmd.sunk | while | flops 1359101952 | bytes 5308675 | solution.py:24
  46.0 0.6 constant_dynamic-slice_fusion.10
  50.2 2.5 fusion.40
  52.8 2.3 fusion.41
  55.8 0.6 constant_dynamic-slice_fusion.10
  60.0 2.5 fusion.40
  62.6 2.3 fusion.41
  65.6 0.6 constant_dynamic-slice_fusion.10
  69.8 2.5 fusion.40
  72.4 2.3 fusion.41
  75.4 0.6 constant_dynamic-slice_fusion.10
  79.6 2.5 fusion.40
  82.1 2.3 fusion.41
  85.2 1.4 copy-done.1
  86.6 32.9 %reduce-scatter.3.cloned.1.call-done = f32[1,384,384]{2,1,0:T(8,128)} async-done(((f32[4,384,384]{2,1,0:T(8,128)}), f32[1,384,384]{2,1,0:T(8,128)}) %reduce-scatter.3.cloned.1.call-update) | async-done | bytes 589840 | tf_op jit(solution)/shard_map/reduce_scatter | solution.py:34
  119.6 76.6 %all-reduce.3.cloned.1.call-done = f32[1,384,384]{2,1,0:T(8,128)} async-done(((f32[1,384,384]{2,1,0:T(8,128)}), f32[1,384,384]{2,1,0:T(8,128)}) %all-reduce.3.cloned.1.call-update) | async-done | bytes 589840 | tf_op jit(solution)/shard_map/psum | solution.py:35
  196.2 1.8 multiply_reduce_fusion.2
  198.0 6.3 %psum.44 = f32[]{:T(128)} all-reduce(f32[]{:T(128)} %multiply_reduce_fusion.2), channel_id=1, replica_groups=mesh['term'=8,'sector'=4] {'sector'}, use_global_device_ids=true, to_apply=%region_7.8 | all-reduce | flops 1 | bytes 8 | tf_op jit(solution)/shard_map/psum | solution.py:28
  204.9 1.9 multiply_reduce_fusion.1
  206.8 7.2 %psum.45 = f32[]{:T(128)} all-reduce(f32[]{:T(128)} %get-tuple-element.122), channel_id=1, replica_groups=mesh['term'=8,'sector'=4] {'sector'}, use_global_device_ids=true, to_apply=%region_9.10 | all-reduce | flops 1 | bytes 8 | tf_op jit(solution)/shard_map/psum | solution.py:28
  214.7 0.9 broadcast_multiply_fusion
  215.7 22.5 %all-gather.5.cloned.1.call-done = f32[4,384,384]{2,1,0:T(8,128)} async-done(((f32[1,384,384]{2,1,0:T(8,128)}), f32[4,384,384]{2,1,0:T(8,128)}) %all-gather.5.cloned.1.call-update) | async-done | bytes 2359312 | tf_op jit(solution)/shard_map/all_gather | solution.py:32
  238.2 0.2 broadcast.6
  238.3 39.8 %while.21 = (s32[]{:T(128)}, f32[4,384,384]{2,1,0:T(8,128)S(1)}, s32[]{:T(128)}, s32[1,4]{1,0:T(1,128)S(1)}, f32[4,384,384]{2,1,0:T(8,128)}, /*index=5*/s32[1,4]...) while((s32[]{:T(128)}, f32[4,384,384]{2,1,0:T(8,128)S(1)}, ...), condition=%wide.region_11.12_spmd, body=%wide.region_10.11_spmd.sunk | while | flops 1359101952 | bytes 5308675 | solution.py:24
  239.0 0.6 constant_dynamic-slice_fusion.12
  243.2 2.5 fusion.46
  245.8 2.3 fusion.47
  248.8 0.6 constant_dynamic-slice_fusion.12
  253.0 2.5 fusion.46
  255.5 2.3 fusion.47
  258.6 0.6 constant_dynamic-slice_fusion.12
  262.8 2.5 fusion.46
  265.3 2.3 fusion.47
  268.3 0.6 constant_dynamic-slice_fusion.12
  272.5 2.5 fusion.46
  275.1 2.3 fusion.47
  278.1 1.4 copy-done
  279.6 32.9 %reduce-scatter.5.cloned.1.call-done = f32[1,384,384]{2,1,0:T(8,128)} async-done(((f32[4,384,384]{2,1,0:T(8,128)}), f32[1,384,384]{2,1,0:T(8,128)}) %reduce-scatter.5.cloned.1.call-update) | async-done | bytes 589840 | tf_op jit(solution)/shard_map/reduce_scatter | solution.py:34
  312.5 76.5 %all-reduce.5.cloned.1.call-done = f32[1,384,384]{2,1,0:T(8,128)} async-done(((f32[1,384,384]{2,1,0:T(8,128)}), f32[1,384,384]{2,1,0:T(8,128)}) %all-reduce.5.cloned.1.call-update) | async-done | bytes 589840 | tf_op jit(solution)/shard_map/psum | solution.py:35
  389.0 1.8 multiply_reduce_fusion
  390.8 6.3 %psum.47 = f32[]{:T(128)} all-reduce(f32[]{:T(128)} %multiply_reduce_fusion), channel_id=1, replica_groups=mesh['term'=8,'sector'=4] {'sector'}, use_global_device_ids=true, to_apply=%region_15.16 | all-reduce | flops 1 | bytes 8 | tf_op jit(solution)/shard_map/psum | solution.py:28
  397.8 0.6 pad_maximum_fusion
  398.3 2.1 divide_subtract_fusion
  (30 shorter events, 0.7 us)
Async XLA Ops:
  7.2 38.2 %copy-start.4 = (s32[1,4]{1,0:T(1,128)S(1)}, s32[1,4]{1,0:T(1,128)}, u32[]{:S(2)}) copy-start(s32[1,4]{1,0:T(1,128)} %param.16) | copy-start | bytes 52
  7.2 38.2 %copy-start.5 = (s32[1,4]{1,0:T(1,128)S(1)}, s32[1,4]{1,0:T(1,128)}, u32[]{:S(2)}) copy-start(s32[1,4]{1,0:T(1,128)} %param.15) | copy-start | bytes 52
  7.2 38.0 %all-gather.3.cloned.1.call-start = ((), (), s32[]{:S(2)}) async-start(), calls=%async_computation.2 | async-start | bytes 2949120 | tf_op jit(solution)/shard_map/all_gather | solution.py:32
  20.7 98.9 %reduce-scatter.3.cloned.1.call-start = ((), (), s32[]{:S(2)}) async-start(), calls=%async_computation.3 | async-start | bytes 2949120 | tf_op jit(solution)/shard_map/reduce_scatter | solution.py:34
  85.1 1.4 copy-start.1
  85.1 111.0 %copy-start.2 = (f32[1,384,384]{2,1,0:T(8,128)S(1)}, f32[1,384,384]{2,1,0:T(8,128)}, u32[]{:S(2)}) copy-start(f32[1,384,384]{2,1,0:T(8,128)} %param.11) | copy-start | bytes 1769476
  85.2 119.8 %copy-start.3 = (f32[1,384,384]{2,1,0:T(8,128)S(1)}, f32[1,384,384]{2,1,0:T(8,128)}, u32[]{:S(2)}) copy-start(f32[1,384,384]{2,1,0:T(8,128)} %param.12) | copy-start | bytes 1769476
  86.6 109.6 %all-reduce.3.cloned.1.call-start = ((), (), s32[]{:S(2)}) async-start(), calls=%async_computation.4 | async-start | bytes 1179648 | tf_op jit(solution)/shard_map/psum | solution.py:35
  119.6 118.6 %all-gather.5.cloned.1.call-start = ((), (), s32[]{:S(2)}) async-start(), calls=%async_computation.5 | async-start | bytes 2949120 | tf_op jit(solution)/shard_map/all_gather | solution.py:32
  215.6 96.9 %reduce-scatter.5.cloned.1.call-start = ((), (), s32[]{:S(2)}) async-start(), calls=%async_computation.6 | async-start | bytes 2949120 | tf_op jit(solution)/shard_map/reduce_scatter | solution.py:34
  278.1 1.4 copy-start
  279.5 109.5 %all-reduce.5.cloned.1.call-start = ((), (), s32[]{:S(2)}) async-start(), calls=%async_computation.7 | async-start | bytes 1179648 | tf_op jit(solution)/shard_map/psum | solution.py:35
Sparse Core Ops, SparseCore 0:
  20.8 24.3 all-gather.2
  86.7 32.8 reduce-scatter.2
  122.9 73.2 all-reduce.2
  215.7 22.4 all-gather.4
  279.7 32.8 reduce-scatter.4
  315.7 73.2 all-reduce.4
where the time goes:
time: 409 us; the launch traced here: 407 us
  waiting for transfers between devices  266 us (65%)
  matrix products  38.7 us (9%)
  loops' own time  35.8 us (9%)
  blocking collectives  28.7 us (7%)
  between operations  16.9 us (4%)
  other arithmetic  12.8 us (3%)
  local copies, waits for them, and re-layouts  8.2 us (2%)
    psum x2, waiting for transfers between devices, sigma_blocks(): return lax.psum(owned_sum, 'term')  153 us
    reduce_scatter x2, waiting for transfers between devices, sigma_blocks(): lax.psum_scatter(partial_value, 'sector', scatter_dimension=0, tiled=True)  65.8 us
    all_gather x2, waiting for transfers between devices, sigma_blocks(): gathered = lax.all_gather(vector, 'sector', axis=0, tiled=True)  47 us
    another operation x2, loops' own time, apply_pairs(): lax.fori_loop(0, pair_count[0], one_pair, jnp.zeros(gathered.shape, jnp.f...  35.8 us
    psum x4, blocking collectives, global_sums(): return lax.psum((values[0],), 'sector')  28.7 us
    dot_general x8, matrix products, one_pair(): inner_prod = jnp.dot(left_block, source, precision=lax.Precision.HIGHEST)  20 us
    dot_general x8, matrix products, one_pair(): lax.dot_general(inner_prod, right_block, (((1,), (1,)), ((), ())), precis...  18.6 us
  transfers between devices with their start and end apart: 6, of which 6 were waited for; matrix products, arithmetic and copies ran while one was open for 0% of the time, Pallas kernels for 0%

commit v1 on v0

--- a/solution.py
+++ b/solution.py
@@ -29,7 +29,20 @@
 
 
 def sigma_blocks(vector, left_ops, right_ops, pair_in, pair_out, pair_count):
-    gathered = lax.all_gather(vector, "sector", axis=0, tiled=True)
+
+    def refer_surface(payload, along_axis):
+        nodes = lax.axis_size(along_axis)
+        val = sorted(((nth, (nth + 1) % nodes) for nth in range(nodes)))
+        response = payload
+        buffer = [response]
+        for tick in tuple(range(1, nodes)):
+            response = lax.ppermute(response, along_axis, val)
+            buffer.insert(0, response)
+        big = jnp.concatenate(buffer, axis=0)
+        reply = lax.axis_index(along_axis) + 1
+        return jnp.roll(big, reply * payload.shape[0], 0)
+
+    gathered = refer_surface(vector, "sector")
     partial_value = apply_pairs(gathered, left_ops, right_ops, pair_in, pair_out, pair_count)
     owned_sum = lax.psum_scatter(partial_value, "sector", scatter_dimension=0, tiled=True)
     return lax.psum(owned_sum, "term")

time: 409 us -> 420 us (1.027)
  waiting for transfers between devices: 266 us -> 273 us
    ppermute x0 -> x6, waiting for transfers between devices: none -> 55.8 us  [refer_surface(): response = lax.ppermute(response, along_axis, val)]
    all_gather x2 -> x0, waiting for transfers between devices: 47 us -> none  [sigma_blocks(): gathered = lax.all_gather(vector, 'sector', axis=0, tiled=True)]
    concatenate x0 -> x2, other arithmetic: none -> 5.42 us  [refer_surface(): return jnp.roll(big, reply * payload.shape[0], 0)]
  transfers between devices with their start and end apart: 6 -> 10, of which waited for: 6 -> 10; matrix products, arithmetic and copies ran while one was open for 0% -> 0% of each run, Pallas kernels for 0% -> 0%
where the time goes in v1:
time: 420 us; the launch traced here: 419 us
  waiting for transfers between devices  273 us (65%)
  matrix products  38.7 us (9%)
  loops' own time  35.5 us (8%)
  blocking collectives  28.7 us (7%)
  other arithmetic  16.7 us (4%)
  between operations  16.5 us (4%)
  local copies, waits for them, and re-layouts  8.76 us (2%)
    psum x2, waiting for transfers between devices, sigma_blocks(): return lax.psum(owned_sum, 'term')  153 us
    reduce_scatter x2, waiting for transfers between devices, sigma_blocks(): lax.psum_scatter(partial_value, 'sector', scatter_dimension=0, tiled=True)  64.3 us
    ppermute x6, waiting for transfers between devices, refer_surface(): response = lax.ppermute(response, along_axis, val)  55.8 us
    another operation x2, loops' own time, apply_pairs(): lax.fori_loop(0, pair_count[0], one_pair, jnp.zeros(gathered.shape, jnp.f...  35.5 us
    psum x4, blocking collectives, global_sums(): return lax.psum((values[0],), 'sector')  28.7 us
    dot_general x8, matrix products, one_pair(): inner_prod = jnp.dot(left_block, source, precision=lax.Precision.HIGHEST)  20.1 us
    dot_general x8, matrix products, one_pair(): lax.dot_general(inner_prod, right_block, (((1,), (1,)), ((), ())), precis...  18.6 us
  transfers between devices with their start and end apart: 10, of which 10 were waited for; matrix products, arithmetic and copies ran while one was open for 0% of the time, Pallas kernels for 0%

profile of v1, /device:TPU:0, one launch (start us, length us, event | category | flops | bytes accessed | tf_op | source)
XLA Modules:
  0.0 418.5 jit_solution(6998843743295864998)
XLA Ops:
  7.2 1.8 multiply_reduce_fusion.3
  9.0 9.0 %psum.42 = f32[]{:T(128)} all-reduce(f32[]{:T(128)} %multiply_reduce_fusion.3), channel_id=1, replica_groups=mesh['term'=8,'sector'=4] {'sector'}, use_global_device_ids=true, to_apply=%region_1.0 | all-reduce | flops 1 | bytes 8 | tf_op jit(solution)/shard_map/psum | solution.py:28
  18.7 1.1 broadcast_multiply_fusion.1
  19.9 9.3 %collective-permute-done = f32[1,384,384]{2,1,0:T(8,128)S(1)} collective-permute-done((f32[1,384,384]{2,1,0:T(8,128)S(1)}, f32[1,384,384]{2,1,0:T(8,128)S(1)}, u32[]{:S(2)}, u32[]{:S(2)}) %collective-permute-start) | collective-permute-done | bytes 589856 | tf_op jit(solution)/shard_map/ppermute | solution.py:39
  29.2 9.3 %collective-permute-done.1 = f32[1,384,384]{2,1,0:T(8,128)S(1)} collective-permute-done((f32[1,384,384]{2,1,0:T(8,128)S(1)}, f32[1,384,384]{2,1,0:T(8,128)S(1)}, u32[]{:S(2)}, u32[]{:S(2)}) %collective-permute-start.1) | collective-permute-done | bytes 589856 | tf_op jit(solution)/shard_map/ppermute | solution.py:39
  38.5 9.3 %collective-permute-done.2 = f32[1,384,384]{2,1,0:T(8,128)S(1)} collective-permute-done((f32[1,384,384]{2,1,0:T(8,128)S(1)}, f32[1,384,384]{2,1,0:T(8,128)S(1)}, u32[]{:S(2)}, u32[]{:S(2)}) %collective-permute-start.2) | collective-permute-done | bytes 589856 | tf_op jit(solution)/shard_map/ppermute | solution.py:39
  47.8 2.7 fusion.32
  51.2 39.8 %while.20 = (s32[]{:T(128)}, f32[4,384,384]{2,1,0:T(8,128)S(1)}, s32[]{:T(128)}, s32[1,4]{1,0:T(1,128)S(1)}, f32[4,384,384]{2,1,0:T(8,128)}, /*index=5*/s32[1,4]...) while((s32[]{:T(128)}, f32[4,384,384]{2,1,0:T(8,128)S(1)}, ...), condition=%wide.region_3.5_spmd, body=%wide.region_2.4_spmd.sunk | while | flops 1359101952 | bytes 5308675 | solution.py:24
  51.9 0.6 constant_dynamic-slice_fusion.10
  56.1 2.5 fusion.54
  58.6 2.3 fusion.55
  61.6 0.6 constant_dynamic-slice_fusion.10
  65.8 2.5 fusion.54
  68.4 2.3 fusion.55
  75.6 2.5 fusion.54
  78.2 2.3 fusion.55
  85.4 2.5 fusion.54
  88.0 2.3 fusion.55
  91.0 1.4 copy-done.1
  92.5 33.2 %reduce-scatter.3.cloned.1.call-done = f32[1,384,384]{2,1,0:T(8,128)} async-done(((f32[4,384,384]{2,1,0:T(8,128)}), f32[1,384,384]{2,1,0:T(8,128)}) %reduce-scatter.3.cloned.1.call-update) | async-done | bytes 589840 | tf_op jit(solution)/shard_map/reduce_scatter | solution.py:47
  125.7 76.6 %all-reduce.3.cloned.1.call-done = f32[1,384,384]{2,1,0:T(8,128)} async-done(((f32[1,384,384]{2,1,0:T(8,128)}), f32[1,384,384]{2,1,0:T(8,128)}) %all-reduce.3.cloned.1.call-update) | async-done | bytes 589840 | tf_op jit(solution)/shard_map/psum | solution.py:48
  202.3 1.8 multiply_reduce_fusion.2
  204.2 6.3 %psum.44 = f32[]{:T(128)} all-reduce(f32[]{:T(128)} %multiply_reduce_fusion.2), channel_id=1, replica_groups=mesh['term'=8,'sector'=4] {'sector'}, use_global_device_ids=true, to_apply=%region_7.9 | all-reduce | flops 1 | bytes 8 | tf_op jit(solution)/shard_map/psum | solution.py:28
  211.1 2.1 multiply_reduce_fusion.1
  213.1 7.2 %psum.45 = f32[]{:T(128)} all-reduce(f32[]{:T(128)} %get-tuple-element.123), channel_id=1, replica_groups=mesh['term'=8,'sector'=4] {'sector'}, use_global_device_ids=true, to_apply=%region_9.11 | all-reduce | flops 1 | bytes 8 | tf_op jit(solution)/shard_map/psum | solution.py:28
  221.2 9.3 %collective-permute-done.3 = f32[1,384,384]{2,1,0:T(8,128)S(1)} collective-permute-done((f32[1,384,384]{2,1,0:T(8,128)S(1)}, f32[1,384,384]{2,1,0:T(8,128)S(1)}, u32[]{:S(2)}, u32[]{:S(2)}) %collective-permute-start.3) | collective-permute-done | bytes 589856 | tf_op jit(solution)/shard_map/ppermute | solution.py:39
  230.4 9.3 %collective-permute-done.4 = f32[1,384,384]{2,1,0:T(8,128)S(1)} collective-permute-done((f32[1,384,384]{2,1,0:T(8,128)S(1)}, f32[1,384,384]{2,1,0:T(8,128)S(1)}, u32[]{:S(2)}, u32[]{:S(2)}) %collective-permute-start.4) | collective-permute-done | bytes 589856 | tf_op jit(solution)/shard_map/ppermute | solution.py:39
  239.8 9.3 %collective-permute-done.5 = f32[1,384,384]{2,1,0:T(8,128)S(1)} collective-permute-done((f32[1,384,384]{2,1,0:T(8,128)S(1)}, f32[1,384,384]{2,1,0:T(8,128)S(1)}, u32[]{:S(2)}, u32[]{:S(2)}) %collective-permute-start.5) | collective-permute-done | bytes 589856 | tf_op jit(solution)/shard_map/ppermute | solution.py:39
  249.1 2.7 fusion.25
  251.9 39.6 %while.21 = (s32[]{:T(128)}, f32[4,384,384]{2,1,0:T(8,128)S(1)}, s32[]{:T(128)}, s32[1,4]{1,0:T(1,128)S(1)}, f32[4,384,384]{2,1,0:T(8,128)}, /*index=5*/s32[1,4]...) while((s32[]{:T(128)}, f32[4,384,384]{2,1,0:T(8,128)S(1)}, ...), condition=%wide.region_11.13_spmd, body=%wide.region_10.12_spmd.sunk | while | flops 1359101952 | bytes 5308675 | solution.py:24
  252.6 0.6 constant_dynamic-slice_fusion.12
  256.8 2.5 fusion.60
  259.3 2.3 fusion.61
  262.3 0.6 constant_dynamic-slice_fusion.12
  266.5 2.5 fusion.60
  269.1 2.3 fusion.61
  272.1 0.6 constant_dynamic-slice_fusion.12
  276.2 2.5 fusion.60
  278.8 2.3 fusion.61
  281.8 0.6 constant_dynamic-slice_fusion.12
  285.9 2.5 fusion.60
  288.5 2.3 fusion.61
  291.5 1.4 copy-done
  293.0 31.1 %reduce-scatter.5.cloned.1.call-done = f32[1,384,384]{2,1,0:T(8,128)} async-done(((f32[4,384,384]{2,1,0:T(8,128)}), f32[1,384,384]{2,1,0:T(8,128)}) %reduce-scatter.5.cloned.1.call-update) | async-done | bytes 589840 | tf_op jit(solution)/shard_map/reduce_scatter | solution.py:47
  324.1 76.5 %all-reduce.5.cloned.1.call-done = f32[1,384,384]{2,1,0:T(8,128)} async-done(((f32[1,384,384]{2,1,0:T(8,128)}), f32[1,384,384]{2,1,0:T(8,128)}) %all-reduce.5.cloned.1.call-update) | async-done | bytes 589840 | tf_op jit(solution)/shard_map/psum | solution.py:48
  400.6 1.8 multiply_reduce_fusion
  402.4 6.3 %psum.47 = f32[]{:T(128)} all-reduce(f32[]{:T(128)} %multiply_reduce_fusion), channel_id=1, replica_groups=mesh['term'=8,'sector'=4] {'sector'}, use_global_device_ids=true, to_apply=%region_15.17 | all-reduce | flops 1 | bytes 8 | tf_op jit(solution)/shard_map/psum | solution.py:28
  409.9 2.1 divide_subtract_fusion
  (38 shorter events, 3.4 us)
Async XLA Ops:
  7.2 118.5 %reduce-scatter.3.cloned.1.call-start = ((), (), s32[]{:S(2)}) async-start(), calls=%async_computation.2 | async-start | bytes 2949120 | tf_op jit(solution)/shard_map/reduce_scatter | solution.py:47
  19.8 9.4 %collective-permute-start = (f32[1,384,384]{2,1,0:T(8,128)S(1)}, f32[1,384,384]{2,1,0:T(8,128)S(1)}, u32[]{:S(2)}, u32[]{:S(2)}) collective-permute-start(f32[1,384,384]{2,1,0:T(8,128)S(1)} %broadcast_multiply_fusion.1), channel_id=1, source_target_pairs={{0,1},{1,2},{2,3},{3,0},{4,5},{5,6},{6,7},{7,4},{8,9},{9,10},{10,1... | collective-permute-start | bytes 1769480 | tf_op jit(solution)/shard_map/ppermute | solution.py:39
  29.2 9.3 %collective-permute-start.1 = (f32[1,384,384]{2,1,0:T(8,128)S(1)}, f32[1,384,384]{2,1,0:T(8,128)S(1)}, u32[]{:S(2)}, u32[]{:S(2)}) collective-permute-start(f32[1,384,384]{2,1,0:T(8,128)S(1)} %collective-permute-done), channel_id=1, source_target_pairs={{0,1},{1,2},{2,3},{3,0},{4,5},{5,6},{6,7},{7,4},{8,9},{9,10},{10,1... | collective-permute-start | bytes 1769480 | tf_op jit(solution)/shard_map/ppermute | solution.py:39
  38.5 9.3 %collective-permute-start.2 = (f32[1,384,384]{2,1,0:T(8,128)S(1)}, f32[1,384,384]{2,1,0:T(8,128)S(1)}, u32[]{:S(2)}, u32[]{:S(2)}) collective-permute-start(f32[1,384,384]{2,1,0:T(8,128)S(1)} %collective-permute-done.1), channel_id=1, source_target_pairs={{0,1},{1,2},{2,3},{3,0},{4,5},{5,6},{6,7},{7,4},{8,9},{9,10},{10,1... | collective-permute-start | bytes 1769480 | tf_op jit(solution)/shard_map/ppermute | solution.py:39
  50.5 0.7 copy-start.4
  50.5 0.7 copy-start.5
  91.0 1.4 copy-start.1
  91.0 111.4 %copy-start.2 = (f32[1,384,384]{2,1,0:T(8,128)S(1)}, f32[1,384,384]{2,1,0:T(8,128)}, u32[]{:S(2)}) copy-start(f32[1,384,384]{2,1,0:T(8,128)} %param.13) | copy-start | bytes 1769476
  92.4 109.9 %all-reduce.3.cloned.1.call-start = ((), (), s32[]{:S(2)}) async-start(), calls=%async_computation.3 | async-start | bytes 1179648 | tf_op jit(solution)/shard_map/psum | solution.py:48
  125.7 198.4 %reduce-scatter.5.cloned.1.call-start = ((), (), s32[]{:S(2)}) async-start(), calls=%async_computation.4 | async-start | bytes 2949120 | tf_op jit(solution)/shard_map/reduce_scatter | solution.py:47
  221.1 9.4 %collective-permute-start.3 = (f32[1,384,384]{2,1,0:T(8,128)S(1)}, f32[1,384,384]{2,1,0:T(8,128)S(1)}, u32[]{:S(2)}, u32[]{:S(2)}) collective-permute-start(f32[1,384,384]{2,1,0:T(8,128)S(1)} %broadcast_multiply_fusion), channel_id=1, source_target_pairs={{0,1},{1,2},{2,3},{3,0},{4,5},{5,6},{6,7},{7,4},{8,9},{9,10},{10,1... | collective-permute-start | bytes 1769480 | tf_op jit(solution)/shard_map/ppermute | solution.py:39
  230.4 9.3 %collective-permute-start.4 = (f32[1,384,384]{2,1,0:T(8,128)S(1)}, f32[1,384,384]{2,1,0:T(8,128)S(1)}, u32[]{:S(2)}, u32[]{:S(2)}) collective-permute-start(f32[1,384,384]{2,1,0:T(8,128)S(1)} %collective-permute-done.3), channel_id=1, source_target_pairs={{0,1},{1,2},{2,3},{3,0},{4,5},{5,6},{6,7},{7,4},{8,9},{9,10},{10,1... | collective-permute-start | bytes 1769480 | tf_op jit(solution)/shard_map/ppermute | solution.py:39
  239.8 9.3 %collective-permute-start.5 = (f32[1,384,384]{2,1,0:T(8,128)S(1)}, f32[1,384,384]{2,1,0:T(8,128)S(1)}, u32[]{:S(2)}, u32[]{:S(2)}) collective-permute-start(f32[1,384,384]{2,1,0:T(8,128)S(1)} %collective-permute-done.4), channel_id=1, source_target_pairs={{0,1},{1,2},{2,3},{3,0},{4,5},{5,6},{6,7},{7,4},{8,9},{9,10},{10,1... | collective-permute-start | bytes 1769480 | tf_op jit(solution)/shard_map/ppermute | solution.py:39
  291.5 1.4 copy-start
  291.5 118.4 %copy-start.3 = (f32[1,384,384]{2,1,0:T(8,128)S(1)}, f32[1,384,384]{2,1,0:T(8,128)}, u32[]{:S(2)}) copy-start(f32[1,384,384]{2,1,0:T(8,128)} %param.14) | copy-start | bytes 1769476
  292.9 107.7 %all-reduce.5.cloned.1.call-start = ((), (), s32[]{:S(2)}) async-start(), calls=%async_computation.5 | async-start | bytes 1179648 | tf_op jit(solution)/shard_map/psum | solution.py:48
Sparse Core Ops, SparseCore 0:
  92.5 33.0 reduce-scatter.2
  129.0 73.2 all-reduce.2
  293.1 31.0 reduce-scatter.4
  327.4 73.2 all-reduce.4
